TPU v7x, 32 devices: a whole 2x2x4 slice. The times are simulated.
32 devices in a mesh: fsdp: 8 (over y, x, core), tensor: 4 (over z).
Axes of the slice: x: 2, y: 2, z: 4, core: 2. Of those that a mesh axis runs over, the one named last changes fastest.
Arguments:
- inputs: bfloat16 [32, 577, 1024], P('fsdp'), may hold values from -6 to 6
- lengths: int32 [32], P('fsdp'), may hold values from 144 to 577, as said below
- norm_gains: bfloat16 [2, 1024], P(None, 'fsdp'), may hold values from 0.5 to 1.5
- norm_shifts: bfloat16 [2, 1024], P(None, 'fsdp'), may hold values from -1.5 to 1.5
- w_qkv: bfloat16 [3, 1024, 1024], P(None, 'fsdp', 'tensor'), may hold values from -0.1875 to 0.1875
- bias_qv: bfloat16 [2, 1024], P(None, 'tensor'), may hold values from -3 to 3
- w_out: bfloat16 [1024, 1024], P('tensor', 'fsdp'), may hold values from -1.5 to 1.5
- out_bias: bfloat16 [2, 1024], P(None, 'fsdp'), may hold values from -1.5 to 1.5
- w_up: bfloat16 [1024, 4096], P('fsdp', 'tensor'), may hold values from -0.1875 to 0.1875
- b_up: bfloat16 [4096], P('tensor'), may hold values from -3 to 3
- w_down: bfloat16 [4096, 1024], P('tensor', 'fsdp'), may hold values from -0.375 to 0.375
- cotangent: bfloat16 [32, 577, 1024], P('fsdp'), may hold values from -6 to 6
Outputs:
- output: bfloat16 [32, 577, 1024], P('fsdp')
- grad_input: float32 [32, 577, 1024], P('fsdp')
- grad_gains: float32 [2, 1024], P(None, 'fsdp')
- grad_shifts: float32 [2, 1024], P(None, 'fsdp')
- grad_qkv: float32 [3, 1024, 1024], P(None, 'fsdp', 'tensor')
- grad_bias_qv: float32 [2, 1024], P(None, 'tensor')
- grad_out: float32 [1024, 1024], P('tensor', 'fsdp')
- grad_out_bias: float32 [2, 1024], P(None, 'fsdp')
- grad_up: float32 [1024, 4096], P('fsdp', 'tensor')
- grad_b_up: float32 [4096], P('tensor')
- grad_down: float32 [4096, 1024], P('tensor', 'fsdp')
Inputs may be any that keep to these rules, and one draw needn't show every extreme that they name: lengths[b] counts the valid leading tokens of image b; some image has all 577 valid and some has 144.
All inputs are finite; a program needn't handle non-finite values.
Results may differ from a plain program's by a relative error of at most 0.02.
Values may be sent and summed in bfloat16 or wider, within the bound.
A program may use at most 256 MiB of HBM per device.

v0:
```python
import jax
import jax.numpy as jnp
from jax import lax
from jax.sharding import PartitionSpec as P

HEAD = 64
epsilon = 1e-06
half_root = 0.7071067811865476
density_scale = 0.3989422804014327


def normalize(tokens):
    average = jnp.mean(tokens, axis=-1, keepdims=True)
    centred = tokens - average
    spread = jnp.mean(centred * centred, axis=-1, keepdims=True)
    inverse = lax.rsqrt(spread + epsilon)
    return (centred * inverse, inverse)


def normalize_back(incoming, normed, inverse, gain):
    scaled = incoming * gain
    return inverse * (
        scaled
        - jnp.mean(scaled, axis=-1, keepdims=True)
        - normed * jnp.mean(scaled * normed, axis=-1, keepdims=True)
    )


def masked_scores(query_heads, key_heads, valid, scale):
    scores = (
        jnp.einsum("bqhe,bkhe->bhqk", query_heads, key_heads, preferred_element_type=jnp.float32)
        * scale
    )
    return jnp.where(valid[:, None, None, :], scores, -jnp.inf)


def local(
    inputs,
    lengths,
    norm_gains,
    norm_shifts,
    w_qkv,
    bias_qv,
    w_out,
    out_bias,
    w_up,
    b_up,
    w_down,
    cotangent,
):
    batch, seq_len, width = inputs.shape
    tokens = batch * seq_len
    local_width = w_qkv.shape[2]
    local_heads = local_width // HEAD
    scale = HEAD ** (-0.5)
    gathered = (
        lax.all_gather(w_qkv, "fsdp", axis=1, tiled=True),
        lax.all_gather(w_out, "fsdp", axis=1, tiled=True),
        lax.all_gather(w_up, "fsdp", axis=0, tiled=True),
        lax.all_gather(w_down, "fsdp", axis=1, tiled=True),
        lax.all_gather(norm_gains, "fsdp", axis=1, tiled=True),
        lax.all_gather(norm_shifts, "fsdp", axis=1, tiled=True),
        lax.all_gather(out_bias, "fsdp", axis=1, tiled=True),
    )
    full_qkv, full_out, full_up, full_down, all_gains, all_shifts, all_bias = gathered
    gain_rows = all_gains.astype(jnp.float32)
    shift_rows = all_shifts.astype(jnp.float32)
    bias_rows = all_bias.astype(jnp.float32)
    proj_bias = bias_qv.astype(jnp.float32)
    hidden_bias = b_up.astype(jnp.float32)
    flat_in = inputs.reshape(tokens, width).astype(jnp.float32)
    normed_one, inverse_one = normalize(flat_in)
    hidden_one = (normed_one * gain_rows[0] + shift_rows[0]).astype(jnp.bfloat16)
    projected = jnp.einsum("rd,cde->cre", hidden_one, full_qkv, preferred_element_type=jnp.float32)
    queries = (projected[0] + proj_bias[0]).astype(jnp.bfloat16)
    key_rows = projected[1].astype(jnp.bfloat16)
    value_rows = (projected[2] + proj_bias[1]).astype(jnp.bfloat16)
    head_shape = (batch, seq_len, local_heads, HEAD)
    query_heads = queries.reshape(head_shape)
    key_heads = key_rows.reshape(head_shape)
    value_heads = value_rows.reshape(head_shape)
    valid = lax.broadcasted_iota(jnp.int32, (batch, seq_len), 1) < lengths[:, None]
    scores = masked_scores(query_heads, key_heads, valid, scale)
    top = jnp.max(scores, axis=-1, keepdims=True)
    log_total = top + jnp.log(jnp.sum(jnp.exp(scores - top), axis=-1, keepdims=True))
    weights_b = jnp.exp(scores - log_total).astype(jnp.bfloat16)
    attended_heads = jnp.einsum(
        "bhqk,bkhe->bqhe", weights_b, value_heads, preferred_element_type=jnp.float32
    ).astype(jnp.bfloat16)
    attended = attended_heads.reshape(tokens, local_width)
    attn_total = lax.psum(
        jnp.dot(attended, full_out, preferred_element_type=jnp.float32).astype(jnp.bfloat16),
        "tensor",
    ).astype(jnp.float32)
    middle = flat_in + (attn_total + bias_rows[0])
    normed_two, inverse_two = normalize(middle)
    hidden_two = (normed_two * gain_rows[1] + shift_rows[1]).astype(jnp.bfloat16)
    before = jnp.dot(hidden_two, full_up, preferred_element_type=jnp.float32) + hidden_bias
    activated = jax.nn.gelu(before, approximate=False).astype(jnp.bfloat16)
    mlp_total = lax.psum(
        jnp.dot(activated, full_down, preferred_element_type=jnp.float32).astype(jnp.bfloat16),
        "tensor",
    ).astype(jnp.float32)
    result = (middle + (mlp_total + bias_rows[1])).astype(jnp.bfloat16)
    back_qkv, back_out, back_up, back_down = (full_qkv, full_out, full_up, full_down)
    grad_rows = cotangent.reshape(tokens, width)
    grad_f = grad_rows.astype(jnp.float32)
    grad_down = jnp.einsum("rf,rd->fd", activated, grad_rows, preferred_element_type=jnp.float32)
    dact = jnp.einsum("rd,fd->rf", grad_rows, back_down, preferred_element_type=jnp.float32)
    normal_cdf = 0.5 * (1.0 + jax.scipy.special.erf(before * half_root))
    density = jnp.exp(-0.5 * before * before) * density_scale
    dbefore = dact * (normal_cdf + before * density)
    dbefore_b = dbefore.astype(jnp.bfloat16)
    grad_b_up = jnp.sum(dbefore, axis=0)
    grad_up = jnp.einsum("rd,rf->df", hidden_two, dbefore_b, preferred_element_type=jnp.float32)
    dhidden_two = lax.psum(
        jnp.einsum("rf,df->rd", dbefore_b, back_up, preferred_element_type=jnp.float32).astype(
            jnp.bfloat16
        ),
        "tensor",
    ).astype(jnp.float32)
    dmiddle = grad_f + normalize_back(dhidden_two, normed_two, inverse_two, gain_rows[1])
    dmiddle_b = dmiddle.astype(jnp.bfloat16)
    grad_out = jnp.einsum("rk,rd->kd", attended, dmiddle_b, preferred_element_type=jnp.float32)
    grad_out_bias = jnp.stack([jnp.sum(dmiddle, axis=0), jnp.sum(grad_f, axis=0)])
    dattended = jnp.einsum(
        "rd,kd->rk", dmiddle_b, back_out, preferred_element_type=jnp.float32
    ).astype(jnp.bfloat16)
    dattended_heads = dattended.reshape(head_shape)
    again_scores = masked_scores(query_heads, key_heads, valid, scale)
    prob = jnp.exp(again_scores - log_total)
    again_weights = prob.astype(jnp.bfloat16)
    dprob = jnp.einsum(
        "bqhe,bkhe->bhqk", dattended_heads, value_heads, preferred_element_type=jnp.float32
    )
    delta = jnp.einsum(
        "bqhe,bqhe->bhq", dattended_heads, attended_heads, preferred_element_type=jnp.float32
    )[..., None]
    dscores = (prob * (dprob - delta) * scale).astype(jnp.bfloat16)
    dqueries = jnp.einsum(
        "bhqk,bkhe->bqhe", dscores, key_heads, preferred_element_type=jnp.float32
    ).reshape(tokens, local_width)
    dkeys = jnp.einsum(
        "bhqk,bqhe->bkhe", dscores, query_heads, preferred_element_type=jnp.float32
    ).reshape(tokens, local_width)
    dvalues = jnp.einsum(
        "bhqk,bqhe->bkhe", again_weights, dattended_heads, preferred_element_type=jnp.float32
    ).reshape(tokens, local_width)
    grad_bias_part = jnp.stack([jnp.sum(dqueries, axis=0), jnp.sum(dvalues, axis=0)])
    stacked = jnp.stack([dqueries, dkeys, dvalues]).astype(jnp.bfloat16)
    grad_qkv = jnp.einsum("rd,cre->cde", hidden_one, stacked, preferred_element_type=jnp.float32)
    dhidden_one = lax.psum(
        jnp.einsum("cre,cde->rd", stacked, back_qkv, preferred_element_type=jnp.float32).astype(
            jnp.bfloat16
        ),
        "tensor",
    ).astype(jnp.float32)
    grad_input = dmiddle + normalize_back(dhidden_one, normed_one, inverse_one, gain_rows[0])
    grad_gains = jnp.stack(
        [jnp.sum(dhidden_one * normed_one, axis=0), jnp.sum(dhidden_two * normed_two, axis=0)]
    )
    grad_shifts = jnp.stack([jnp.sum(dhidden_one, axis=0), jnp.sum(dhidden_two, axis=0)])
    owned_qkv, owned_out, owned_up, owned_down, owned_gains, owned_shifts, owned_bias = (
        lax.psum_scatter(
            grad_qkv.astype(jnp.bfloat16), "fsdp", scatter_dimension=1, tiled=True
        ).astype(jnp.float32),
        lax.psum_scatter(
            grad_out.astype(jnp.bfloat16), "fsdp", scatter_dimension=1, tiled=True
        ).astype(jnp.float32),
        lax.psum_scatter(
            grad_up.astype(jnp.bfloat16), "fsdp", scatter_dimension=0, tiled=True
        ).astype(jnp.float32),
        lax.psum_scatter(
            grad_down.astype(jnp.bfloat16), "fsdp", scatter_dimension=1, tiled=True
        ).astype(jnp.float32),
        lax.psum_scatter(
            grad_gains.astype(jnp.bfloat16), "fsdp", scatter_dimension=1, tiled=True
        ).astype(jnp.float32),
        lax.psum_scatter(
            grad_shifts.astype(jnp.bfloat16), "fsdp", scatter_dimension=1, tiled=True
        ).astype(jnp.float32),
        lax.psum_scatter(
            grad_out_bias.astype(jnp.bfloat16), "fsdp", scatter_dimension=1, tiled=True
        ).astype(jnp.float32),
    )
    summed_bias_qv, summed_b_up = lax.psum((grad_bias_part, grad_b_up), "fsdp")
    return (
        result.reshape(batch, seq_len, width),
        grad_input.reshape(batch, seq_len, width),
        owned_gains,
        owned_shifts,
        owned_qkv,
        summed_bias_qv,
        owned_out,
        owned_bias,
        owned_up,
        summed_b_up,
        owned_down,
    )


def solution(mesh):
    placed = (
        P("fsdp", None, None),
        P("fsdp"),
        P(None, "fsdp"),
        P(None, "fsdp"),
        P(None, "fsdp", "tensor"),
        P(None, "tensor"),
        P("tensor", "fsdp"),
        P(None, "fsdp"),
        P("fsdp", "tensor"),
        P("tensor"),
        P("tensor", "fsdp"),
        P("fsdp", None, None),
    )
    return jax.shard_map(
        local,
        mesh=mesh,
        in_specs=placed,
        out_specs=(
            P("fsdp", None, None),
            P("fsdp", None, None),
            P(None, "fsdp"),
            P(None, "fsdp"),
            P(None, "fsdp", "tensor"),
            P(None, "tensor"),
            P("tensor", "fsdp"),
            P(None, "fsdp"),
            P("fsdp", "tensor"),
            P("tensor"),
            P("tensor", "fsdp"),
        ),
        check_vma=False,
    )
```

profile of v0, /device:TPU:0, one launch (start us, length us, event | category | flops | bytes accessed | tf_op | source)
XLA Modules:
  0.0 1187.7 jit_solution(13304505593827600482)
XLA Ops:
  8.8 7.8 copy.100
  18.8 5.8 multiply_reduce_fusion.1
  24.9 8.4 reshape.154
  33.3 10.2 all_gather.21
  43.5 8.8 all_gather.22
  52.3 9.5 all_gather.24
  62.0 7.9 convolution_bitcast_fusion
  78.5 4.6 reshape.175
  89.8 4.3 squeeze.7
  99.1 10.7 fusion.1
  109.8 11.2 exponential_reduce_fusion
  121.1 10.8 convolution_convert_fusion.7
  139.9 8.8 all_gather.25
  149.3 6.1 copy.112
  155.4 5.8 reshape.151
  161.2 150.4 %all-reduce.6.cloned.1.call-done = bf16[2308,1024]{1,0:T(8,128)(2,1)} async-done(((bf16[2308,1024]{1,0:T(8,128)(2,1)}), bf16[2308,1024]{1,0:T(8,128)(2,1)}) %all-reduce.6.cloned.1.call-update) | async-done | bytes 4726800 | tf_op jit(solution)/shard_map/psum | solution.py:91
  311.6 10.0 fusion.66
  321.6 4.8 multiply_reduce_fusion
  326.4 13.9 %all-gather.6.cloned.1.call-done = bf16[1024,1024]{1,0:T(8,128)(2,1)} async-done(((bf16[128,1024]{1,0:T(8,128)(2,1)}), bf16[1024,1024]{1,0:T(8,128)(2,1)}) %all-gather.6.cloned.1.call-update) | async-done | bytes 2097168 | tf_op jit(solution)/shard_map/all_gather | solution.py:59
  340.3 30.0 %fusion.20 = (bf16[2308,1024]{1,0:T(8,128)(2,1)}, f32[2308,1024]{1,0:T(8,128)}) fusion(f32[1024]{0:T(1024)S(1)} %convert_element_type.159, bf16[1024,1024]{1,0:T(8,128)(2,1)} %all-gather.6.cloned.1.call-done, f32[2308,1024]{1,0:T(8,128)} %get-tuple-element.70, f32[1024]{0:T(1024)S(1)} %bitcast.111, f32[1024]{0:T(1024)S(1)} %bitcast.100, ...), kind=kOutput, calls=%fused_computation.30 | convolution fusion | flops 5008027648 | bytes 25761824 | tf_op jit(solution)/shard_map/dot_general | solution.py:98
  370.3 12.2 %fusion.71 = (f32[1024]{0:T(1024)}, bf16[2308,1024]{1,0:T(8,128)(2,1)S(1)}) fusion(f32[2308,1024]{1,0:T(8,128)} %get-tuple-element.82, f32[1024]{0:T(1024)S(1)} %convert_element_type.159, bf16[2308,1024]{1,0:T(8,128)(2,1)} %reshape.151, bf16[1024,1024]{1,0:T(8,128)(2,1)} %all-gather.8.cloned.1.call-done), kind=kOutput, calls=%fused_computation.127 | convolution fusion | flops 4868586496 | bytes 21012480 | tf_op jit(solution)/shard_map/rd,fd->rf/dot_general | solution.py:109
  384.8 6.8 convolution_convert_fusion
  391.6 9.3 convolution_convert_fusion.4
  403.6 4.3 reduce.7
  407.9 13.2 %fusion.40 = bf16[1024,1024]{1,0:T(8,128)(2,1)} fusion(bf16[2308,1024]{1,0:T(8,128)(2,1)} %copy-done.39, f32[2308,1024]{1,0:T(8,128)} %get-tuple-element.70, f32[1024]{0:T(1024)S(1)} %bitcast.112, f32[1024]{0:T(1024)S(1)} %bitcast.101, f32[2308]{0:T(1024)S(1)} %add_rsqrt_fusion.1, f32[2308]{0:T(1024)S(1)} %broadcast_multiply_fusion.5), kind=kOutput, calls=%fused_computation.81 | convolution fusion | flops 4853092352 | bytes 16304160 | tf_op jit(solution)/shard_map/rd,rf->df/dot_general | solution.py:115
  421.1 143.2 %all-reduce.8.cloned.1.call-done = bf16[2308,1024]{1,0:T(8,128)(2,1)} async-done(((bf16[2308,1024]{1,0:T(8,128)(2,1)}), bf16[2308,1024]{1,0:T(8,128)(2,1)}) %all-reduce.8.cloned.1.call-update) | async-done | bytes 4726800 | tf_op jit(solution)/shard_map/psum | solution.py:116
  564.4 9.2 fusion.12
  573.6 7.8 fusion.64
  593.1 17.2 %multiply_convert_fusion = bf16[4,4,577,577]{2,3,1,0:T(8,128)(2,1)} fusion(f32[4,4,577,577]{2,3,1,0:T(8,128)} %get-tuple-element.80, f32[4,4,577]{2,1,0:T(4,128)S(1)} %multiply_reduce_fusion.2, f32[4,4,577]{2,1,0:T(4,128)S(1)} %bitcast.94, pred[4,577]{1,0:T(4,128)(4,1)S(1)} %copy-done.21, bf16[4,577,4,64]{1,0,3,2:T(4,128)(2,1)} %reshape.152, ...), kind=kOutput, calls=%fused_computation | convolution fusion | flops 719126592 | bytes 34400740 | tf_op jit(solution)/shard_map/bqhe,bkhe->bhqk/dot_general | solution.py:133
  610.3 8.7 bitcast_convert_fusion.2
  619.9 4.2 copy.143
  627.9 9.6 fusion.44
  637.5 12.5 %bitcast_convert_fusion.1 = (bf16[4,577,4,64]{1,3,2,0:T(8,128)(2,1)}, f32[4,4,64,577]{3,2,1,0:T(8,128)}) fusion(f32[4,4,577,577]{2,3,1,0:T(8,128)} %get-tuple-element.80, f32[4,4,577]{2,1,0:T(4,128)S(1)} %bitcast.95, pred[4,577]{1,0:T(4,128)(4,1)S(1)} %copy-done.21, bf16[4,577,4,64]{1,0,3,2:T(4,128)(2,1)S(1)} %copy-done.11), kind=kOutput, calls=%fused_computation.68 | convolution fusion | flops 703736896 | bytes 26073476 | tf_op jit(solution)/shard_map/bhqk,bqhe->bkhe/dot_general | solution.py:146
  665.8 10.9 fusion.43
  681.5 9.5 convolution_convert_fusion.1
  691.0 5.5 bitcast_convert_fusion
  706.2 13.9 %all-reduce = (f32[2,256]{1,0:T(2,128)}, f32[1024]{0:T(1024)}) all-reduce(f32[2,256]{1,0:T(2,128)S(1)} %pad_maximum_fusion.3, f32[1024]{0:T(1024)S(1)} %copy-done.29), channel_id=1, replica_groups=mesh['fsdp'=8,'tensor'=4] {'fsdp'}, use_global_device_ids=true, to_apply=%region_23.24 | all-reduce | flops 1536 | bytes 12288 | tf_op jit(solution)/shard_map/psum | solution.py:186
  721.5 5.3 reduce-scatter.28.cloned.1.call-done
  728.3 39.9 %reduce-scatter.26.cloned.1.call-done = bf16[128,768]{1,0:T(8,128)(2,1)} async-done(((bf16[1024,768]{1,0:T(8,128)(2,1)}), bf16[128,768]{1,0:T(8,128)(2,1)}) %reduce-scatter.26.cloned.1.call-update) | async-done | bytes 196624
  770.3 327.2 %all-reduce.10.cloned.1.call-done = (bf16[2308,1024]{1,0:T(8,128)(2,1)}, bf16[2308,1024]{1,0:T(8,128)(2,1)}) async-done(((bf16[2308,1024]{1,0:T(8,128)(2,1)}, bf16[2308,1024]{1,0:T(8,128)(2,1)}), (bf16[2308,1024]{1,0:T(8,128)(2,1)}, bf16[2308,1024]{1,0:T(8,128)(2,1)})) %all-reduce.10.cloned.1.call-update) | async-done | bytes 9453584 | tf_op jit(solution)/shard_map/psum | solution.py:100
  1100.6 8.4 fusion.17
  1110.1 13.2 %fusion.15 = f32[2308,1024]{1,0:T(8,128)} fusion(f32[2308,1024]{1,0:T(8,128)} %copy-done, bf16[2308,1024]{1,0:T(8,128)(2,1)} %get-tuple-element.66, f32[2308,1024]{1,0:T(8,128)} %reshape.154, f32[2308]{0:T(1024)S(1)} %broadcast_multiply_fusion.1, f32[2308]{0:T(1024)S(1)} %broadcast_multiply_fusion.2, f32[1024]{0:T(1024)S(1)} %bitcast.99, ...), kind=kLoop, calls=%fused_computation.25 | loop fusion | flops 21270528 | bytes 33128512 | tf_op jit(solution)/shard_map/add | solution.py:158
  1124.3 9.0 add_convert_fusion
  1133.3 5.8 reshape.150
  1139.1 8.2 copy.129
  1147.3 8.4 reshape.153
  1155.7 13.8 %copy.130 = f32[4,577,1024]{2,0,1:T(4,128)} copy(f32[4,577,1024]{2,1,0:T(8,128)} %reshape.153) | data formatting | bytes 18907136
  1171.0 8.6 reduce-scatter.24.cloned.1.call-done
  (201 shorter events, 97.5 us)
Async XLA Ops:
  7.2 9.5 slice-start
  7.2 54.8 %all-gather.4.cloned.1.call-start = ((), (), s32[]{:S(2)}) async-start(), calls=%async_computation.7 | async-start | bytes 1769472 | tf_op jit(solution)/shard_map/all_gather | solution.py:57
  7.9 303.7 %all-reduce.6.cloned.1.call-start = ((), (), s32[]{:S(2)}) async-start(), calls=%async_computation.8 | async-start | bytes 9469952 | tf_op jit(solution)/shard_map/psum | solution.py:91
  8.8 7.9 slice-start.1
  24.8 37.1 %copy-start.16 = (f32[2308]{0:T(1024)}, f32[2308]{0:T(1024)S(1)}, u32[]{:S(2)}) copy-start(f32[2308]{0:T(1024)S(1)} %rsqrt.20) | copy-start | bytes 27700
  24.9 37.1 %copy-start.18 = (f32[2308]{0:T(1024)}, f32[2308]{0:T(1024)S(1)}, u32[]{:S(2)}) copy-start(f32[2308]{0:T(1024)S(1)} %div.27) | copy-start | bytes 27700
  24.9 8.5 copy-start.33
  24.9 18.6 %copy-start.34 = (bf16[2,128]{1,0:T(2,128)(2,1)S(1)}, bf16[2,128]{1,0:T(2,128)(2,1)}, u32[]{:S(2)}) copy-start(bf16[2,128]{1,0:T(2,128)(2,1)} %param.15) | copy-start | bytes 1540
  24.9 27.4 %copy-start.22 = (bf16[256,128]{1,0:T(8,128)(2,1)S(1)}, bf16[256,128]{1,0:T(8,128)(2,1)}, u32[]{:S(2)}) copy-start(bf16[256,128]{1,0:T(8,128)(2,1)} %param.18) | copy-start | bytes 196612
  24.9 36.9 %copy-start.36 = (s32[4]{0:T(128)S(1)}, s32[4]{0:T(128)}, u32[]{:S(2)}) copy-start(s32[4]{0:T(128)} %param.13) | copy-start | bytes 52
  61.8 73.2 %copy-start.12 = (bf16[256,1024]{1,0:T(8,128)(2,1)}, bf16[256,1024]{1,0:T(8,128)(2,1)S(1)}, u32[]{:S(2)}) copy-start(bf16[256,1024]{1,0:T(8,128)(2,1)S(1)} %all_gather.24) | copy-start | bytes 1572868
  61.9 59.2 %copy-start.20 = (pred[4,577]{1,0:T(4,128)(4,1)}, pred[4,577]{1,0:T(4,128)(4,1)S(1)}, u32[]{:S(2)}) copy-start(pred[4,577]{1,0:T(4,128)(4,1)S(1)} %iota_compare_fusion) | copy-start | bytes 6928
  61.9 8.0 copy-start.30
  61.9 8.0 copy-start.25
  86.2 23.6 %copy-start.6 = (bf16[4,577,4,64]{1,3,2,0:T(8,128)(2,1)}, bf16[4,577,4,64]{1,3,2,0:T(8,128)(2,1)S(1)}, u32[]{:S(2)}) copy-start(bf16[4,577,4,64]{1,3,2,0:T(8,128)(2,1)S(1)} %copy.108) | copy-start | bytes 3545092
  96.4 13.5 %copy-start.2 = (bf16[4,577,4,64]{1,0,3,2:T(4,128)(2,1)}, bf16[4,577,4,64]{1,0,3,2:T(4,128)(2,1)S(1)}, u32[]{:S(2)}) copy-start(bf16[4,577,4,64]{1,0,3,2:T(4,128)(2,1)S(1)} %add_convert_fusion.3) | copy-start | bytes 3545092
  99.1 22.0 %copy-start.14 = (bf16[4,577,4,64]{1,0,3,2:T(4,128)(2,1)}, bf16[4,577,4,64]{1,0,3,2:T(4,128)(2,1)S(1)}, u32[]{:S(2)}) copy-start(bf16[4,577,4,64]{1,0,3,2:T(4,128)(2,1)S(1)} %add_convert_fusion.4) | copy-start | bytes 3545092
  121.1 10.8 copy-start.23
  135.0 20.4 %copy-start.4 = (bf16[2308,256]{0,1:T(8,128)(2,1)}, bf16[2308,256]{0,1:T(8,128)(2,1)S(1)}, u32[]{:S(2)}) copy-start(bf16[2308,256]{0,1:T(8,128)(2,1)S(1)} %reshape.149) | copy-start | bytes 3545092
  138.5 201.7 %all-gather.6.cloned.1.call-start = ((), (), s32[]{:S(2)}) async-start(), calls=%async_computation.9 | async-start | bytes 2359296 | tf_op jit(solution)/shard_map/all_gather | solution.py:59
  139.3 231.0 %all-gather.8.cloned.1.call-start = ((), (), s32[]{:S(2)}) async-start(), calls=%async_computation.10 | async-start | bytes 2359296 | tf_op jit(solution)/shard_map/all_gather | solution.py:60
  139.9 424.5 %all-reduce.8.cloned.1.call-start = ((), (), s32[]{:S(2)}) async-start(), calls=%async_computation.11 | async-start | bytes 9469952 | tf_op jit(solution)/shard_map/psum | solution.py:116
  370.3 14.4 %copy-start.37 = (bf16[1024,1024]{1,0:T(8,128)(2,1)S(1)}, bf16[1024,1024]{1,0:T(8,128)(2,1)}, u32[]{:S(2)}) copy-start(bf16[1024,1024]{1,0:T(8,128)(2,1)} %all-gather.6.cloned.1.call-done) | copy-start | bytes 6291460
  391.5 305.1 %reduce-scatter.32.cloned.1.call-start = ((), (), s32[]{:S(2)}) async-start(), calls=%async_computation.18 | async-start | bytes 2359296
  403.6 295.2 %reduce-scatter.20.cloned.1.call-start = ((), (), s32[]{:S(2)}) async-start(), calls=%async_computation.12 | async-start | bytes 2359296 | tf_op jit(solution)/shard_map/reduce_scatter | solution.py:170
  421.1 298.9 %reduce-scatter.30.cloned.1.call-start = ((), (), s32[]{:S(2)}) async-start(), calls=%async_computation.17 | async-start | bytes 294912
  564.4 9.2 copy-start.1
  573.6 7.8 copy-start.5
  583.2 9.5 copy-start.10
  585.2 7.8 copy-start.21
  585.2 7.8 copy-start.24
  593.1 17.2 %copy-start.7 = (bf16[4,577,4,64]{1,3,2,0:T(8,128)(2,1)S(1)}, bf16[4,577,4,64]{1,3,2,0:T(8,128)(2,1)}, u32[]{:S(2)}) copy-start(bf16[4,577,4,64]{1,3,2,0:T(8,128)(2,1)} %copy-done.6) | copy-start | bytes 3545092
  610.3 17.6 %copy-start.3 = (bf16[4,577,4,64]{1,0,3,2:T(4,128)(2,1)S(1)}, bf16[4,577,4,64]{1,0,3,2:T(4,128)(2,1)}, u32[]{:S(2)}) copy-start(bf16[4,577,4,64]{1,0,3,2:T(4,128)(2,1)} %copy-done.2) | copy-start | bytes 3545092
  627.9 9.6 copy-start.11
  650.0 76.7 %reduce-scatter.28.cloned.1.call-start = ((), (), s32[]{:S(2)}) async-start(), calls=%async_computation.16 | async-start | bytes 589824
  652.1 13.7 %copy-start.26 = (f32[1,1024]{1,0:T(1,128)S(1)}, f32[1,1024]{1,0:T(1,128)}, u32[]{:S(2)}) copy-start(f32[1,1024]{1,0:T(1,128)} %copy-done.25) | copy-start | bytes 12292
  652.1 13.7 %copy-start.31 = (f32[1,1024]{1,0:T(1,128)S(1)}, f32[1,1024]{1,0:T(1,128)}, u32[]{:S(2)}) copy-start(f32[1,1024]{1,0:T(1,128)} %copy-done.30) | copy-start | bytes 12292
  662.3 105.9 %reduce-scatter.26.cloned.1.call-start = ((), (), s32[]{:S(2)}) async-start(), calls=%async_computation.15 | async-start | bytes 1769472
  681.4 9.6 copy-start.15
  681.4 416.1 %all-reduce.10.cloned.1.call-start = ((), (), s32[]{:S(2)}) async-start(), calls=%async_computation.19 | async-start | bytes 18939904 | tf_op jit(solution)/shard_map/psum | solution.py:100
  681.5 9.5 copy-start.38
  696.6 9.3 copy-start.8
  696.6 9.6 copy-start.29
  696.6 404.0 %copy-start.17 = (f32[2308]{0:T(1024)S(1)}, f32[2308]{0:T(1024)}, u32[]{:S(2)}) copy-start(f32[2308]{0:T(1024)} %copy-done.16) | copy-start | bytes 27700
  696.6 404.0 %copy-start.19 = (f32[2308]{0:T(1024)S(1)}, f32[2308]{0:T(1024)}, u32[]{:S(2)}) copy-start(f32[2308]{0:T(1024)} %copy-done.18) | copy-start | bytes 27700
  696.6 472.9 %reduce-scatter.22.cloned.1.call-start = ((), (), s32[]{:S(2)}) async-start(), calls=%async_computation.13 | async-start | bytes 294912
  1110.0 14.3 %copy-start.27 = (f32[1,1024]{1,0:T(1,128)S(1)}, f32[1,1024]{1,0:T(1,128)}, u32[]{:S(2)}) copy-start(f32[1,1024]{1,0:T(1,128)} %get-tuple-element.73) | copy-start | bytes 12292
  1110.0 69.5 %reduce-scatter.24.cloned.1.call-start = ((), (), s32[]{:S(2)}) async-start(), calls=%async_computation.14 | async-start | bytes 294912
  (7 other events, 29.9 us)
Sparse Core Ops, SparseCore 0:
  9.9 28.2 all-gather.3
  138.7 172.9 all-reduce.5
  313.5 26.7 all-gather.5
  342.0 28.0 all-gather.7
  391.7 172.6 all-reduce.7
  567.5 40.0 reduce-scatter.31
  610.9 41.1 reduce-scatter.19
  655.6 33.7 reduce-scatter.29
  692.5 34.2 reduce-scatter.27
  729.9 38.3 reduce-scatter.25
  771.4 326.0 all-reduce.9
  1110.1 32.6 reduce-scatter.21
  1145.8 33.6 reduce-scatter.23
where the time goes:
time: 1200 us; the launch traced here: 1190 us
  waiting for transfers between devices  691 us (58%)
  matrix products  182 us (15%)
  local copies, waits for them, and re-layouts  142 us (12%)
  other arithmetic  107 us (9%)
  blocking collectives  51.1 us (4%)
  between operations  14.9 us (1%)
    psum x1, waiting for transfers between devices, local(): lax.psum(jnp.dot(activated, full_down, preferred_element_type=jnp.float32...  327 us
    psum x1, waiting for transfers between devices, local(): lax.psum(jnp.dot(attended, full_out, preferred_element_type=jnp.float32)....  150 us
    psum x1, waiting for transfers between devices, local(): lax.psum(jnp.einsum('rf,df->rd', dbefore_b, back_up, preferred_element_ty...  143 us
    unnamed x19, waiting for transfers between devices  55.8 us
    unnamed x106, local copies, waits for them, and re-layouts  53.4 us
    dot_general x1, matrix products, local(): jnp.dot(hidden_two, full_up, preferred_element_type=jnp.float32)  30 us
  transfers between devices with their start and end apart: 13, of which 7 were waited for; matrix products, arithmetic and copies ran while one was open for 27% of the time, Pallas kernels for 0%

commit v1 on v0

--- a/solution.py
+++ b/solution.py
@@ -7,6 +7,10 @@
 epsilon = 1e-06
 half_root = 0.7071067811865476
 density_scale = 0.3989422804014327
+
+
+def lead_records(incoming_x):
+    return jnp.sum(lax.all_gather(incoming_x, "tensor"), axis=0)
 
 
 def normalize(tokens):
@@ -97,9 +101,8 @@
     hidden_two = (normed_two * gain_rows[1] + shift_rows[1]).astype(jnp.bfloat16)
     before = jnp.dot(hidden_two, full_up, preferred_element_type=jnp.float32) + hidden_bias
     activated = jax.nn.gelu(before, approximate=False).astype(jnp.bfloat16)
-    mlp_total = lax.psum(
-        jnp.dot(activated, full_down, preferred_element_type=jnp.float32).astype(jnp.bfloat16),
-        "tensor",
+    mlp_total = lead_records(
+        jnp.dot(activated, full_down, preferred_element_type=jnp.float32).astype(jnp.bfloat16)
     ).astype(jnp.float32)
     result = (middle + (mlp_total + bias_rows[1])).astype(jnp.bfloat16)
     back_qkv, back_out, back_up, back_down = (full_qkv, full_out, full_up, full_down)

time: 1200 us -> 1370 us (1.14)
  waiting for transfers between devices: 691 us -> 851 us
    all_gather x0 -> x1, waiting for transfers between devices: none -> 316 us  [lead_records(): return jnp.sum(lax.all_gather(incoming_x, 'tensor'), axis=0)]
    psum x1, waiting for transfers between devices: 327 us -> 173 us  [local(): lax.psum(jnp.einsum('cre,cde->rd', stacked, back_qkv, preferred_element_t...]
    reduce_sum x0 -> x1, other arithmetic: none -> 16.7 us  [lead_records(): return jnp.sum(lax.all_gather(incoming_x, 'tensor'), axis=0)]
    unnamed x19 -> x20, waiting for transfers between devices: 55.8 us -> 64.6 us
    unnamed x106 -> x98, local copies, waits for them, and re-layouts: 53.4 us -> 53.1 us
  transfers between devices with their start and end apart: 13 -> 14, of which waited for: 7 -> 7; matrix products, arithmetic and copies ran while one was open for 27% -> 24% of each run, Pallas kernels for 0% -> 0%
where the time goes in v1:
time: 1370 us; the launch traced here: 1360 us
  waiting for transfers between devices  851 us (62%)
  matrix products  184 us (13%)
  local copies, waits for them, and re-layouts  141 us (10%)
  other arithmetic  119 us (9%)
  blocking collectives  51.8 us (4%)
  between operations  14.8 us (1%)
    all_gather x1, waiting for transfers between devices, lead_records(): return jnp.sum(lax.all_gather(incoming_x, 'tensor'), axis=0)  316 us
    psum x1, waiting for transfers between devices, local(): lax.psum(jnp.einsum('cre,cde->rd', stacked, back_qkv, preferred_element_t...  173 us
    psum x1, waiting for transfers between devices, local(): lax.psum(jnp.dot(attended, full_out, preferred_element_type=jnp.float32)....  150 us
    psum x1, waiting for transfers between devices, local(): lax.psum(jnp.einsum('rf,df->rd', dbefore_b, back_up, preferred_element_ty...  134 us
    unnamed x20, waiting for transfers between devices  64.6 us
    unnamed x98, local copies, waits for them, and re-layouts  53.1 us
    dot_general x1, matrix products, local(): jnp.dot(hidden_two, full_up, preferred_element_type=jnp.float32)  30 us
  transfers between devices with their start and end apart: 14, of which 7 were waited for; matrix products, arithmetic and copies ran while one was open for 24% of the time, Pallas kernels for 0%

profile of v1, /device:TPU:0, one launch (start us, length us, event | category | flops | bytes accessed | tf_op | source)
XLA Modules:
  0.0 1362.6 jit_solution(15563754438792900226)
XLA Ops:
  8.8 7.8 copy.100
  18.7 5.8 multiply_reduce_fusion.1
  24.9 8.4 reshape.154
  33.4 10.2 all_gather.27
  43.5 8.8 all_gather.28
  52.3 9.5 all_gather.30
  61.9 7.9 convolution_bitcast_fusion
  78.4 4.6 reshape.179
  89.8 4.3 squeeze.7
  99.1 10.7 fusion.1
  109.8 11.2 exponential_reduce_fusion
  121.0 10.8 convolution_convert_fusion.7
  139.9 8.8 all_gather.31
  149.3 6.1 copy.112
  155.4 5.7 reshape.151
  161.1 150.5 %all-reduce.5.cloned.1.call-done = bf16[2308,1024]{1,0:T(8,128)(2,1)} async-done(((bf16[2308,1024]{1,0:T(8,128)(2,1)}), bf16[2308,1024]{1,0:T(8,128)(2,1)}) %all-reduce.5.cloned.1.call-update) | async-done | bytes 4726800 | tf_op jit(solution)/shard_map/psum | solution.py:95
  311.6 10.1 fusion.67
  321.7 4.8 multiply_reduce_fusion
  326.5 13.8 %all-gather.9.cloned.1.call-done = bf16[1024,1024]{1,0:T(8,128)(2,1)} async-done(((bf16[128,1024]{1,0:T(8,128)(2,1)}), bf16[1024,1024]{1,0:T(8,128)(2,1)}) %all-gather.9.cloned.1.call-update) | async-done | bytes 2097168 | tf_op jit(solution)/shard_map/all_gather | solution.py:63
  340.3 30.0 %fusion.20 = (bf16[2308,1024]{1,0:T(8,128)(2,1)}, f32[2308,1024]{1,0:T(8,128)}) fusion(f32[1024]{0:T(1024)S(1)} %convert_element_type.161, bf16[1024,1024]{1,0:T(8,128)(2,1)} %all-gather.9.cloned.1.call-done, f32[2308,1024]{1,0:T(8,128)} %get-tuple-element.68, f32[1024]{0:T(1024)S(1)} %bitcast.113, f32[1024]{0:T(1024)S(1)} %bitcast.102, ...), kind=kOutput, calls=%fused_computation.30 | convolution fusion | flops 5008027648 | bytes 25761824 | tf_op jit(solution)/shard_map/dot_general | solution.py:102
  370.3 12.2 fusion.72
  384.8 6.8 convolution_convert_fusion
  391.7 9.5 fusion.33
  401.3 8.9 convolution_convert_fusion.4
  412.9 4.3 reduce.8
  417.2 13.2 fusion.41
  430.7 133.8 %all-reduce.7.cloned.1.call-done = bf16[2308,1024]{1,0:T(8,128)(2,1)} async-done(((bf16[2308,1024]{1,0:T(8,128)(2,1)}), bf16[2308,1024]{1,0:T(8,128)(2,1)}) %all-reduce.7.cloned.1.call-update) | async-done | bytes 4726800 | tf_op jit(solution)/shard_map/psum | solution.py:119
  564.5 8.4 fusion.12
  572.8 315.7 %all-gather.13.cloned.1.call-done = bf16[4,2308,1024]{2,1,0:T(8,128)(2,1)} async-done(((bf16[1,2308,1024]{2,1,0:T(8,128)(2,1)}), bf16[4,2308,1024]{2,1,0:T(8,128)(2,1)}) %all-gather.13.cloned.1.call-update) | async-done | bytes 18907152 | tf_op jit(solution)/shard_map/all_gather | solution.py:13
  888.5 16.7 %reduce_sum.179 = bf16[2308,1024]{1,0:T(8,128)(2,1)} reduce(bf16[4,2308,1024]{2,1,0:T(8,128)(2,1)} %all-gather.13.cloned.1.call-done, bf16[]{:T(256)} %constant.80.clone.1), dimensions={0}, to_apply=%region_7.8 | reduce | flops 7090176 | bytes 23633922 | tf_op jit(solution)/shard_map/reduce_sum | solution.py:13
  905.3 12.5 fusion.65
  929.3 17.2 %multiply_convert_fusion = bf16[4,4,577,577]{2,3,1,0:T(8,128)(2,1)} fusion(f32[4,4,577,577]{2,3,1,0:T(8,128)} %get-tuple-element.79, f32[4,4,577]{2,1,0:T(4,128)S(1)} %multiply_reduce_fusion.2, f32[4,4,577]{2,1,0:T(4,128)S(1)} %bitcast.96, pred[4,577]{1,0:T(4,128)(4,1)S(1)} %copy-done.19, bf16[4,577,4,64]{1,0,3,2:T(4,128)(2,1)} %reshape.152, ...), kind=kOutput, calls=%fused_computation | convolution fusion | flops 719126592 | bytes 34400740 | tf_op jit(solution)/shard_map/bqhe,bkhe->bhqk/dot_general | solution.py:136
  946.5 8.8 bitcast_convert_fusion.2
  956.2 4.2 copy.143
  964.2 9.2 fusion.45
  973.4 12.4 bitcast_convert_fusion.1
  1001.7 10.9 fusion.44
  1017.3 8.6 bitcast_convert_fusion
  1035.5 5.8 reshape.150
  1041.2 8.2 copy.129
  1049.5 14.6 %all-reduce = (f32[2,256]{1,0:T(2,128)}, f32[1024]{0:T(1024)}) all-reduce(f32[2,256]{1,0:T(2,128)S(1)} %pad_maximum_fusion.3, f32[1024]{0:T(1024)S(1)} %copy-done.26), channel_id=1, replica_groups=mesh['fsdp'=8,'tensor'=4] {'fsdp'}, use_global_device_ids=true, to_apply=%region_23.24 | all-reduce | flops 1536 | bytes 12288 | tf_op jit(solution)/shard_map/psum | solution.py:189
  1067.2 30.4 %reduce-scatter.26.cloned.1.call-done = bf16[128,768]{1,0:T(8,128)(2,1)} async-done(((bf16[1024,768]{1,0:T(8,128)(2,1)}), bf16[128,768]{1,0:T(8,128)(2,1)}) %reduce-scatter.26.cloned.1.call-update) | async-done | bytes 196624
  1099.7 172.8 %all-reduce.9.cloned.1.call-done = bf16[2308,1024]{1,0:T(8,128)(2,1)} async-done(((bf16[2308,1024]{1,0:T(8,128)(2,1)}), bf16[2308,1024]{1,0:T(8,128)(2,1)}) %all-reduce.9.cloned.1.call-update) | async-done | bytes 4726800 | tf_op jit(solution)/shard_map/psum | solution.py:155
  1275.6 8.4 fusion.17
  1285.9 13.0 fusion.15
  1299.0 8.4 reshape.153
  1307.4 13.6 copy.130
  1322.3 32.1 %reduce-scatter.24.cloned.1.call-done = bf16[128,2]{1,0:T(8,128)(2,1)} async-done(((bf16[1024,2]{1,0:T(8,128)(2,1)}), bf16[128,2]{1,0:T(8,128)(2,1)}) %reduce-scatter.24.cloned.1.call-update) | async-done | bytes 528
  (196 shorter events, 97.6 us)
Async XLA Ops:
  7.2 9.5 slice-start
  7.2 54.7 %all-gather.7.cloned.1.call-start = ((), (), s32[]{:S(2)}) async-start(), calls=%async_computation.7 | async-start | bytes 1769472 | tf_op jit(solution)/shard_map/all_gather | solution.py:61
  7.9 303.7 %all-reduce.5.cloned.1.call-start = ((), (), s32[]{:S(2)}) async-start(), calls=%async_computation.8 | async-start | bytes 9469952 | tf_op jit(solution)/shard_map/psum | solution.py:95
  8.8 7.8 slice-start.1
  24.8 37.1 %copy-start.14 = (f32[2308]{0:T(1024)}, f32[2308]{0:T(1024)S(1)}, u32[]{:S(2)}) copy-start(f32[2308]{0:T(1024)S(1)} %rsqrt.20) | copy-start | bytes 27700
  24.9 37.0 %copy-start.16 = (f32[2308]{0:T(1024)}, f32[2308]{0:T(1024)S(1)}, u32[]{:S(2)}) copy-start(f32[2308]{0:T(1024)S(1)} %div.27) | copy-start | bytes 27700
  24.9 8.5 copy-start.29
  24.9 18.7 %copy-start.30 = (bf16[2,128]{1,0:T(2,128)(2,1)S(1)}, bf16[2,128]{1,0:T(2,128)(2,1)}, u32[]{:S(2)}) copy-start(bf16[2,128]{1,0:T(2,128)(2,1)} %param.15) | copy-start | bytes 1540
  24.9 27.4 %copy-start.20 = (bf16[256,128]{1,0:T(8,128)(2,1)S(1)}, bf16[256,128]{1,0:T(8,128)(2,1)}, u32[]{:S(2)}) copy-start(bf16[256,128]{1,0:T(8,128)(2,1)} %param.18) | copy-start | bytes 196612
  24.9 36.8 %copy-start.32 = (s32[4]{0:T(128)S(1)}, s32[4]{0:T(128)}, u32[]{:S(2)}) copy-start(s32[4]{0:T(128)} %param.13) | copy-start | bytes 52
  61.7 73.2 %copy-start.11 = (bf16[256,1024]{1,0:T(8,128)(2,1)}, bf16[256,1024]{1,0:T(8,128)(2,1)S(1)}, u32[]{:S(2)}) copy-start(bf16[256,1024]{1,0:T(8,128)(2,1)S(1)} %all_gather.30) | copy-start | bytes 1572868
  61.8 59.2 %copy-start.18 = (pred[4,577]{1,0:T(4,128)(4,1)}, pred[4,577]{1,0:T(4,128)(4,1)S(1)}, u32[]{:S(2)}) copy-start(pred[4,577]{1,0:T(4,128)(4,1)S(1)} %iota_compare_fusion) | copy-start | bytes 6928
  61.8 8.0 copy-start.27
  61.9 8.0 copy-start.23
  86.1 23.6 %copy-start.5 = (bf16[4,577,4,64]{1,3,2,0:T(8,128)(2,1)}, bf16[4,577,4,64]{1,3,2,0:T(8,128)(2,1)S(1)}, u32[]{:S(2)}) copy-start(bf16[4,577,4,64]{1,3,2,0:T(8,128)(2,1)S(1)} %copy.108) | copy-start | bytes 3545092
  96.3 13.5 copy-start.1
  99.1 22.0 %copy-start.13 = (bf16[4,577,4,64]{1,0,3,2:T(4,128)(2,1)}, bf16[4,577,4,64]{1,0,3,2:T(4,128)(2,1)S(1)}, u32[]{:S(2)}) copy-start(bf16[4,577,4,64]{1,0,3,2:T(4,128)(2,1)S(1)} %add_convert_fusion.4) | copy-start | bytes 3545092
  121.0 10.8 copy-start.21
  132.9 7.0 copy-start.28
  132.9 7.0 copy-start.31
  134.9 20.5 %copy-start.3 = (bf16[2308,256]{0,1:T(8,128)(2,1)}, bf16[2308,256]{0,1:T(8,128)(2,1)S(1)}, u32[]{:S(2)}) copy-start(bf16[2308,256]{0,1:T(8,128)(2,1)S(1)} %reshape.149) | copy-start | bytes 3545092
  138.5 201.7 %all-gather.9.cloned.1.call-start = ((), (), s32[]{:S(2)}) async-start(), calls=%async_computation.9 | async-start | bytes 2359296 | tf_op jit(solution)/shard_map/all_gather | solution.py:63
  139.3 231.0 %all-gather.11.cloned.1.call-start = ((), (), s32[]{:S(2)}) async-start(), calls=%async_computation.10 | async-start | bytes 2359296 | tf_op jit(solution)/shard_map/all_gather | solution.py:64
  139.8 424.6 %all-reduce.7.cloned.1.call-start = ((), (), s32[]{:S(2)}) async-start(), calls=%async_computation.11 | async-start | bytes 9469952 | tf_op jit(solution)/shard_map/psum | solution.py:119
  370.3 14.5 %copy-start.34 = (bf16[1024,1024]{1,0:T(8,128)(2,1)S(1)}, bf16[1024,1024]{1,0:T(8,128)(2,1)}, u32[]{:S(2)}) copy-start(bf16[1024,1024]{1,0:T(8,128)(2,1)} %all-gather.9.cloned.1.call-done) | copy-start | bytes 6291460
  384.8 6.9 copy-start.33
  391.6 496.9 %all-gather.13.cloned.1.call-start = ((), (), s32[]{:S(2)}) async-start(), calls=%async_computation.14 | async-start | bytes 23674880 | tf_op jit(solution)/shard_map/all_gather | solution.py:13
  401.3 624.7 %reduce-scatter.32.cloned.1.call-start = ((), (), s32[]{:S(2)}) async-start(), calls=%async_computation.20 | async-start | bytes 2359296
  412.9 615.2 %reduce-scatter.20.cloned.1.call-start = ((), (), s32[]{:S(2)}) async-start(), calls=%async_computation.13 | async-start | bytes 2359296 | tf_op jit(solution)/shard_map/reduce_scatter | solution.py:173
  430.4 633.7 %reduce-scatter.30.cloned.1.call-start = ((), (), s32[]{:S(2)}) async-start(), calls=%async_computation.19 | async-start | bytes 294912
  572.8 332.5 %copy-start.25 = (f32[1,1024]{1,0:T(1,128)S(1)}, f32[1,1024]{1,0:T(1,128)}, u32[]{:S(2)}) copy-start(f32[1,1024]{1,0:T(1,128)} %get-tuple-element.72) | copy-start | bytes 12292
  905.3 12.5 copy-start.4
  919.5 9.4 copy-start.9
  921.6 7.6 copy-start.19
  921.6 7.6 copy-start.22
  929.3 17.2 %copy-start.6 = (bf16[4,577,4,64]{1,3,2,0:T(8,128)(2,1)S(1)}, bf16[4,577,4,64]{1,3,2,0:T(8,128)(2,1)}, u32[]{:S(2)}) copy-start(bf16[4,577,4,64]{1,3,2,0:T(8,128)(2,1)} %copy-done.5) | copy-start | bytes 3545092
  946.5 17.7 %copy-start.2 = (bf16[4,577,4,64]{1,0,3,2:T(4,128)(2,1)S(1)}, bf16[4,577,4,64]{1,0,3,2:T(4,128)(2,1)}, u32[]{:S(2)}) copy-start(bf16[4,577,4,64]{1,0,3,2:T(4,128)(2,1)} %copy-done.1) | copy-start | bytes 3545092
  964.2 9.2 copy-start.10
  985.8 79.7 %reduce-scatter.28.cloned.1.call-start = ((), (), s32[]{:S(2)}) async-start(), calls=%async_computation.18 | async-start | bytes 589824
  988.0 13.7 %copy-start.24 = (f32[1,1024]{1,0:T(1,128)S(1)}, f32[1,1024]{1,0:T(1,128)}, u32[]{:S(2)}) copy-start(f32[1,1024]{1,0:T(1,128)} %copy-done.23) | copy-start | bytes 12292
  998.2 99.4 %reduce-scatter.26.cloned.1.call-start = ((), (), s32[]{:S(2)}) async-start(), calls=%async_computation.17 | async-start | bytes 1769472
  1017.1 255.4 %all-reduce.9.cloned.1.call-start = ((), (), s32[]{:S(2)}) async-start(), calls=%async_computation.12 | async-start | bytes 9469952 | tf_op jit(solution)/shard_map/psum | solution.py:155
  1025.9 9.3 copy-start.7
  1025.9 295.0 %reduce-scatter.22.cloned.1.call-start = ((), (), s32[]{:S(2)}) async-start(), calls=%async_computation.15 | async-start | bytes 294912
  1035.5 14.0 %copy-start.26 = (f32[1024]{0:T(1024)S(1)}, f32[1024]{0:T(1024)}, u32[]{:S(2)}) copy-start(f32[1024]{0:T(1024)} %get-tuple-element.86) | copy-start | bytes 12292
  1041.2 234.4 %copy-start.15 = (f32[2308]{0:T(1024)S(1)}, f32[2308]{0:T(1024)}, u32[]{:S(2)}) copy-start(f32[2308]{0:T(1024)} %copy-done.14) | copy-start | bytes 27700
  1041.2 234.4 %copy-start.17 = (f32[2308]{0:T(1024)S(1)}, f32[2308]{0:T(1024)}, u32[]{:S(2)}) copy-start(f32[2308]{0:T(1024)} %copy-done.16) | copy-start | bytes 27700
  1285.0 69.4 %reduce-scatter.24.cloned.1.call-start = ((), (), s32[]{:S(2)}) async-start(), calls=%async_computation.16 | async-start | bytes 294912
  (4 other events, 8.9 us)
Sparse Core Ops, SparseCore 0:
  9.9 28.2 all-gather.6
  138.6 172.8 all-reduce.4
  313.5 26.7 all-gather.8
  342.0 28.0 all-gather.10
  391.8 172.6 all-reduce.6
  565.9 322.5 all-gather.12
  891.8 39.9 reduce-scatter.31
  935.1 41.1 reduce-scatter.19
  986.0 32.8 reduce-scatter.29
  1021.8 34.0 reduce-scatter.27
  1059.2 38.3 reduce-scatter.25
  1099.8 172.6 all-reduce.8
  1285.1 32.6 reduce-scatter.21
  1320.7 33.7 reduce-scatter.23
